TPU v7x, 32 devices: a whole 2x2x4 slice. The times are simulated.
32 devices in a mesh: tm: 8 (over z, x), rows: 4 (over y, core).
Axes of the slice: x: 2, y: 2, z: 4, core: 2. Of those that a mesh axis runs over, the one named last changes fastest.
Arguments:
- frames: bfloat16 [8, 32, 64, 128], P('tm', 'rows'), may hold values from -6 to 6
- decays: float32 [8, 256], P('tm'), may hold values from 0.4 to 1
- in_weight: bfloat16 [3, 3, 128, 256], replicated, may hold values from -0.046875 to 0.046875
- out_weight: bfloat16 [3, 3, 256, 128], replicated, may hold values from -0.125 to 0.125
- skip_gain: float32 [128], replicated, may hold values from 0.25 to 1.75
- cotangent: bfloat16 [8, 32, 64, 128], P('tm', 'rows'), may hold values from -6 to 6
Outputs:
- output_frames: bfloat16 [8, 32, 64, 128], P('tm', 'rows')
- input_grad: bfloat16 [8, 32, 64, 128], P('tm', 'rows')
- in_weight_grad: float32 [3, 3, 128, 256], replicated
- out_weight_grad: float32 [3, 3, 256, 128], replicated
- gain_grad: float32 [128], replicated
- decay_grad: float32 [8, 256], P('tm')
All inputs are finite; a program needn't handle non-finite values.
Results may differ from a plain program's by a relative error of at most 0.008.
Values may be sent and summed in bfloat16 or wider, within the bound.
A program may use at most 192 MiB of HBM per device.

v0:
```python
import math
import jax
import jax.numpy as jnp
from jax import lax
from jax.sharding import PartitionSpec as P


def padded_2(block, sides, width):
    for axis, dim in sides:
        count = lax.axis_size(axis)
        forward = [(i, i + 1) for i in range(count - 1)]
        backward = [(target, source) for source, target in forward]
        low = lax.ppermute(
            lax.slice_in_dim(block, block.shape[dim] - width, None, axis=dim), axis, forward
        )
        high = lax.ppermute(lax.slice_in_dim(block, 0, width, axis=dim), axis, backward)
        block = jnp.concatenate([low, block, high], axis=dim)
    return block


def entering(array, axis, join, neutral, backward):
    count = lax.axis_size(axis)
    place = lax.axis_index(axis)
    ahead = count - 1 - place if backward else place
    gathered = jax.tree.map(
        lambda a, kind: lax.all_gather(a.astype(kind), axis), array, (jnp.bfloat16, jnp.bfloat16)
    )
    state = jax.tree.map(lambda a, e: jnp.zeros_like(a) + jnp.asarray(e, a.dtype), array, neutral)

    def one(turn, state):
        source = count - 1 - turn if backward else turn
        return join(
            state,
            jax.tree.map(
                lambda a, own: lax.dynamic_index_in_dim(a, source, 0, False).astype(own.dtype),
                gathered,
                array,
            ),
        )

    return lax.fori_loop(0, ahead, one, state)


def pad_columns(padded_rows):
    return jnp.pad(padded_rows, ((0, 0), (0, 0), (1, 1), (0, 0)))


def conv_taps(padded, weights):
    frame_count = padded.shape[0]
    height = padded.shape[1] - 2
    across = padded.shape[2] - 2
    channels = padded.shape[3]
    result = jnp.zeros((frame_count * height * across, weights.shape[3]), jnp.float32)
    for row_tap in range(3):
        for col_tap in range(3):
            window = padded[:, row_tap : row_tap + height, col_tap : col_tap + across, :].reshape(
                -1, channels
            )
            result = result + jnp.dot(
                window, weights[row_tap, col_tap], preferred_element_type=jnp.float32
            )
    return result.reshape(frame_count, height, across, weights.shape[3])


def tap_grads(padded, grad_field):
    height = grad_field.shape[1]
    across = grad_field.shape[2]
    channels = padded.shape[3]
    flat_grad = grad_field.reshape(-1, grad_field.shape[3])
    outer_list = []
    for row_tap in range(3):
        inner_list = []
        for col_tap in range(3):
            window = padded[:, row_tap : row_tap + height, col_tap : col_tap + across, :].reshape(
                -1, channels
            )
            inner_list.append(
                lax.dot_general(
                    window, flat_grad, (((0,), (0,)), ((), ())), preferred_element_type=jnp.float32
                )
            )
        outer_list.append(jnp.stack(inner_list))
    return jnp.stack(outer_list)


def flipped(weights):
    return jnp.transpose(weights[::-1, ::-1], (0, 1, 3, 2))


def combine(earlier, later):
    return (earlier[0] * later[0], later[0][None, None, :] * earlier[1] + later[1])


def on_device(frames, decays, in_weight, out_weight, skip_gain, cotangent):
    frame_count, band_rows, across, channels = frames.shape
    states_width = in_weight.shape[3]
    total_frames = frame_count * lax.axis_size("tm")
    total_rows = band_rows * lax.axis_size("rows")
    cell_norm = 1.0 / math.sqrt(total_frames * total_rows * across)
    frame_norm = 1.0 / math.sqrt(total_rows * across)
    in_pad = pad_columns(padded_2(frames, (("rows", 1),), 1))
    drive_terms = conv_taps(in_pad, in_weight)

    def forward_step(state, inputs):
        decay_now, drive_now = inputs
        state = decay_now[None, None, :] * state + drive_now
        return (state, state)

    zero_state = jnp.zeros((band_rows, across, states_width), jnp.float32)
    _, local_states = lax.scan(forward_step, zero_state, (decays, drive_terms))
    decay_prefix = jnp.cumprod(decays, axis=0)
    identity = (jnp.ones((states_width,), jnp.float32), zero_state)
    carried = entering((decay_prefix[-1], local_states[-1]), "tm", combine, identity, False)[1]
    states = local_states + decay_prefix[:, None, None, :] * carried[None]
    rounded = states.astype(jnp.bfloat16)
    state_pad = pad_columns(padded_2(rounded, (("rows", 1),), 1))
    output_frames = (
        conv_taps(state_pad, out_weight) + skip_gain * frames.astype(jnp.float32)
    ).astype(jnp.bfloat16)
    cot_pad = pad_columns(padded_2(cotangent, (("rows", 1),), 1))
    from_output = conv_taps(cot_pad, flipped(out_weight))
    next_decay = jnp.concatenate([decays[1:], jnp.zeros((1, states_width), jnp.float32)], axis=0)

    def backward_step(adjoint_now, inputs):
        decay_next, from_now = inputs
        adjoint_now = from_now + decay_next[None, None, :] * adjoint_now
        return (adjoint_now, adjoint_now)

    _, local_adjoint = lax.scan(backward_step, zero_state, (next_decay, from_output), reverse=True)
    later_decay = jnp.concatenate([decays[1:], jnp.ones((1, states_width), jnp.float32)], axis=0)
    decay_suffix = jnp.cumprod(later_decay[::-1], axis=0)[::-1]
    leading = decays[0][None, None, :] * local_adjoint[0]
    incoming = entering((decay_prefix[-1], leading), "tm", combine, identity, True)[1]
    adjoint = local_adjoint + decay_suffix[:, None, None, :] * incoming[None]
    previous = jnp.concatenate([carried[None], states[:-1]], axis=0)
    decay_terms = jnp.sum(adjoint * previous, axis=(1, 2)) * frame_norm
    adjoint_low = adjoint.astype(jnp.bfloat16)
    in_grad_terms = tap_grads(in_pad, adjoint_low) * cell_norm
    out_grad_terms = tap_grads(state_pad, cotangent) * cell_norm
    gain_terms = (
        jnp.sum(cotangent.astype(jnp.float32) * frames.astype(jnp.float32), axis=(0, 1, 2))
        * cell_norm
    )
    adjoint_pad = pad_columns(padded_2(adjoint_low, (("rows", 1),), 1))
    input_grad = (
        conv_taps(adjoint_pad, flipped(in_weight)) + skip_gain * cotangent.astype(jnp.float32)
    ).astype(jnp.bfloat16)
    in_weight_grad, out_weight_grad, gain_grad = lax.psum(
        (in_grad_terms, out_grad_terms, gain_terms), ("tm", "rows")
    )
    decay_grad = lax.psum(decay_terms, "rows")
    return (output_frames, input_grad, in_weight_grad, out_weight_grad, gain_grad, decay_grad)


def solution(mesh):
    in_specs = (
        P("tm", "rows", None, None),
        P("tm", None),
        P(),
        P(),
        P(),
        P("tm", "rows", None, None),
    )
    out_specs = (
        P("tm", "rows", None, None),
        P("tm", "rows", None, None),
        P(),
        P(),
        P(),
        P("tm", None),
    )
    return jax.shard_map(
        on_device, mesh=mesh, in_specs=in_specs, out_specs=out_specs, check_vma=False
    )
```

profile of v0, /device:TPU:0, one launch (start us, length us, event | category | flops | bytes accessed | tf_op | source)
XLA Modules:
  0.0 304.3 jit_solution(4210442601135215782)
XLA Ops:
  8.0 1.3 collective-permute-start.1
  9.3 3.0 collective-permute-start
  17.4 1.3 collective-permute-start.5
  18.8 5.1 %collective-permute-start.4 = (bf16[1,1,64,128]{3,2,1,0:T(8,128)(2,1)S(1)}, bf16[1,1,64,128]{3,2,1,0:T(8,128)(2,1)S(1)}, u32[]{:S(2)}, u32[]{:S(2)}) collective-permute-start(bf16[1,1,64,128]{3,2,1,0:T(8,128)(2,1)S(1)} %get-tuple-element.225), channel_id=1, source_target_pairs={{0,1},{1,2},{2,3},{4,5},{5,6},{6,7},{8,9},{9,10},{10,11},{12,13},{... | collective-permute-start | bytes 49160 | tf_op jit(solution)/shard_map/ppermute | solution.py:13
  28.4 20.8 %all-gather = bf16[8,1,256]{2,1,0:T(2,128)(2,1)S(1)} all-gather(bf16[1,1,256]{2,1,0:T(2,128)(2,1)S(1)} %convert_bitcast_fusion), channel_id=1, replica_groups=mesh['tm'=8,'rows'=4] {'tm'}, dimensions={0}, use_global_device_ids=true | all-gather | bytes 4608 | tf_op jit(solution)/shard_map/all_gather | solution.py:26
  50.1 21.5 %all-gather.4.cloned.1.call-done = bf16[8,8,64,256]{3,2,1,0:T(8,128)(2,1)} async-done(((bf16[1,8,64,256]{3,2,1,0:T(8,128)(2,1)}), bf16[8,8,64,256]{3,2,1,0:T(8,128)(2,1)}) %all-gather.4.cloned.1.call-update) | async-done | bytes 2097168 | tf_op jit(solution)/shard_map/all_gather | solution.py:26
  71.6 49.9 %all-gather.6.cloned.1.call-done = bf16[8,8,64,256]{3,2,1,0:T(8,128)(2,1)} async-done(((bf16[1,8,64,256]{3,2,1,0:T(8,128)(2,1)}), bf16[8,8,64,256]{3,2,1,0:T(8,128)(2,1)}) %all-gather.6.cloned.1.call-update) | async-done | bytes 2097168 | tf_op jit(solution)/shard_map/all_gather | solution.py:26
  121.5 8.5 %while.17 = (s32[]{:T(128)}, f32[8,64,256]{2,1,0:T(8,128)S(1)}, s32[]{:T(128)}, bf16[8,256]{1,0:T(8,128)(2,1)S(1)}, bf16[8,8,64,256]{3,2,1,0:T(8,128)(2,1)}, /*index=5*/s32[]{:T(128)}, s32[]{:T(128)}, s32[]{:T(128)}, s32[]{:T(128)}) while((s32[]{:T(128)}, f32[8,64,256]{2,1,0:T(8,128)S(1)}, s32[]{:T(128)}, bf16[8,256]{1,0:T(8,128)(2,1)S(1)}, ...), condition=%wide.region_4.5_spmd, body=%wide.region_3.4_spmd.sunk | while | flops 393478 | bytes 1313435 | solution.py:41
  121.6 1.2 convert_add_fusion.5
  122.8 1.2 convert_add_fusion.5
  124.0 1.2 convert_add_fusion.5
  125.2 1.2 convert_add_fusion.5
  126.4 1.2 convert_add_fusion.5
  127.6 1.2 convert_add_fusion.5
  128.9 1.2 convert_add_fusion.5
  132.4 1.3 collective-permute-start.7
  133.7 3.0 collective-permute-start.6
  137.0 1.3 collective-permute-start.3
  138.3 3.6 %collective-permute-start.2 = (bf16[1,1,64,256]{3,2,1,0:T(8,128)(2,1)S(1)}, bf16[1,1,64,256]{3,2,1,0:T(8,128)(2,1)S(1)}, u32[]{:S(2)}, u32[]{:S(2)}) collective-permute-start(bf16[1,1,64,256]{3,2,1,0:T(8,128)(2,1)S(1)} %get-tuple-element.206), channel_id=1, source_target_pairs={{0,1},{1,2},{2,3},{4,5},{5,6},{6,7},{8,9},{9,10},{10,11},{12,13},{... | collective-permute-start | bytes 98312 | tf_op jit(solution)/shard_map/ppermute | solution.py:13
  142.0 1.1 maximum_multiply_fusion
  143.2 7.9 %psum.31 = f32[1,256]{1,0:T(1,128)} all-reduce(f32[1,256]{1,0:T(1,128)S(1)} %bitcast.421), channel_id=1, replica_groups=mesh['tm'=8,'rows'=4] {'rows'}, use_global_device_ids=true, to_apply=%region_10.11 | all-reduce | flops 256 | bytes 2048 | tf_op jit(solution)/shard_map/psum | solution.py:151
  163.2 37.1 %psum.30 = f32[128]{0:T(128)} all-reduce(f32[128]{0:T(128)S(1)} %broadcast_multiply_fusion.2), channel_id=1, replica_groups=mesh['tm'=8,'rows'=4] {'tm','rows'}, use_global_device_ids=true, to_apply=%region_8.9 | all-reduce | flops 128 | bytes 1024 | tf_op jit(solution)/shard_map/psum | solution.py:148
  200.3 94.0 %all-reduce.7.cloned.1.call-done = (f32[3,3,128,256]{3,2,1,0:T(8,128)}, f32[3,3,256,128]{3,2,1,0:T(8,128)}) async-done(((f32[3,3,128,256]{3,2,1,0:T(8,128)}, f32[3,3,256,128]{3,2,1,0:T(8,128)}), (f32[3,3,128,256]{3,2,1,0:T(8,128)}, f32[3,3,256,128]{3,2,1,0:T(8,128)})) %all-reduce.7.cloned.1.call-update) | async-done | bytes 2359312 | tf_op jit(solution)/shard_map/psum | solution.py:148
  294.3 2.5 copy.34
  (134 shorter events, 26.7 us)
Async XLA Ops:
  7.2 7.1 %copy-start.2 = (bf16[3,3,128,256]{3,2,1,0:T(8,128)(2,1)S(1)}, bf16[3,3,128,256]{3,2,1,0:T(8,128)(2,1)}, u32[]{:S(2)}) copy-start(bf16[3,3,128,256]{3,2,1,0:T(8,128)(2,1)} %param.12) | copy-start | bytes 1769476
  7.2 64.4 %all-gather.4.cloned.1.call-start = ((), (), s32[]{:S(2)}) async-start(), calls=%async_computation | async-start | bytes 2359296 | tf_op jit(solution)/shard_map/all_gather | solution.py:26
  8.0 5.0 %collective-permute-start.1 = (bf16[1,1,64,128]{3,2,1,0:T(8,128)(2,1)S(1)}, bf16[1,1,64,128]{3,2,1,0:T(8,128)(2,1)S(1)}, u32[]{:S(2)}, u32[]{:S(2)}) collective-permute-start(bf16[1,1,64,128]{3,2,1,0:T(8,128)(2,1)S(1)} %get-tuple-element.230), channel_id=1, source_target_pairs={{1,0},{2,1},{3,2},{5,4},{6,5},{7,6},{9,8},{10,9},{11,10},{13,12},{... | collective-permute-start | bytes 49160 | tf_op jit(solution)/shard_map/ppermute | solution.py:16
  9.3 3.9 %collective-permute-start = (bf16[1,1,64,128]{3,2,1,0:T(8,128)(2,1)S(1)}, bf16[1,1,64,128]{3,2,1,0:T(8,128)(2,1)S(1)}, u32[]{:S(2)}, u32[]{:S(2)}) collective-permute-start(bf16[1,1,64,128]{3,2,1,0:T(8,128)(2,1)S(1)} %get-tuple-element.229), channel_id=1, source_target_pairs={{0,1},{1,2},{2,3},{4,5},{5,6},{6,7},{8,9},{9,10},{10,11},{12,13},{... | collective-permute-start | bytes 49160 | tf_op jit(solution)/shard_map/ppermute | solution.py:13
  14.1 0.9 copy-start.1
  16.4 1.1 copy-start
  16.4 7.5 %copy-start.3 = (bf16[3,3,256,128]{3,2,1,0:T(8,128)(2,1)S(1)}, bf16[3,3,256,128]{3,2,1,0:T(8,128)(2,1)}, u32[]{:S(2)}) copy-start(bf16[3,3,256,128]{3,2,1,0:T(8,128)(2,1)} %param.13) | copy-start | bytes 1769476
  17.4 104.1 %all-gather.6.cloned.1.call-start = ((), (), s32[]{:S(2)}) async-start(), calls=%async_computation.1 | async-start | bytes 2359296 | tf_op jit(solution)/shard_map/all_gather | solution.py:26
  17.4 6.5 %collective-permute-start.5 = (bf16[1,1,64,128]{3,2,1,0:T(8,128)(2,1)S(1)}, bf16[1,1,64,128]{3,2,1,0:T(8,128)(2,1)S(1)}, u32[]{:S(2)}, u32[]{:S(2)}) collective-permute-start(bf16[1,1,64,128]{3,2,1,0:T(8,128)(2,1)S(1)} %get-tuple-element.226), channel_id=1, source_target_pairs={{1,0},{2,1},{3,2},{5,4},{6,5},{7,6},{9,8},{10,9},{11,10},{13,12},{... | collective-permute-start | bytes 49160 | tf_op jit(solution)/shard_map/ppermute | solution.py:16
  18.8 6.0 %collective-permute-start.4 = (bf16[1,1,64,128]{3,2,1,0:T(8,128)(2,1)S(1)}, bf16[1,1,64,128]{3,2,1,0:T(8,128)(2,1)S(1)}, u32[]{:S(2)}, u32[]{:S(2)}) collective-permute-start(bf16[1,1,64,128]{3,2,1,0:T(8,128)(2,1)S(1)} %get-tuple-element.225), channel_id=1, source_target_pairs={{0,1},{1,2},{2,3},{4,5},{5,6},{6,7},{8,9},{9,10},{10,11},{12,13},{... | collective-permute-start | bytes 49160 | tf_op jit(solution)/shard_map/ppermute | solution.py:13
  26.8 0.7 copy-start.9
  28.3 266.0 %all-reduce.7.cloned.1.call-start = ((), (), s32[]{:S(2)}) async-start(), calls=%async_computation.2 | async-start | bytes 4718592 | tf_op jit(solution)/shard_map/psum | solution.py:148
  132.4 20.7 %collective-permute-start.7 = (bf16[1,1,64,256]{3,2,1,0:T(8,128)(2,1)S(1)}, bf16[1,1,64,256]{3,2,1,0:T(8,128)(2,1)S(1)}, u32[]{:S(2)}, u32[]{:S(2)}) collective-permute-start(bf16[1,1,64,256]{3,2,1,0:T(8,128)(2,1)S(1)} %get-tuple-element.203), channel_id=1, source_target_pairs={{1,0},{2,1},{3,2},{5,4},{6,5},{7,6},{9,8},{10,9},{11,10},{13,12},{... | collective-permute-start | bytes 98312 | tf_op jit(solution)/shard_map/ppermute | solution.py:16
  133.7 19.4 %collective-permute-start.6 = (bf16[1,1,64,256]{3,2,1,0:T(8,128)(2,1)S(1)}, bf16[1,1,64,256]{3,2,1,0:T(8,128)(2,1)S(1)}, u32[]{:S(2)}, u32[]{:S(2)}) collective-permute-start(bf16[1,1,64,256]{3,2,1,0:T(8,128)(2,1)S(1)} %get-tuple-element.202), channel_id=1, source_target_pairs={{0,1},{1,2},{2,3},{4,5},{5,6},{6,7},{8,9},{9,10},{10,11},{12,13},{... | collective-permute-start | bytes 98312 | tf_op jit(solution)/shard_map/ppermute | solution.py:13
  137.0 14.1 %collective-permute-start.3 = (bf16[1,1,64,256]{3,2,1,0:T(8,128)(2,1)S(1)}, bf16[1,1,64,256]{3,2,1,0:T(8,128)(2,1)S(1)}, u32[]{:S(2)}, u32[]{:S(2)}) collective-permute-start(bf16[1,1,64,256]{3,2,1,0:T(8,128)(2,1)S(1)} %get-tuple-element.207), channel_id=1, source_target_pairs={{1,0},{2,1},{3,2},{5,4},{6,5},{7,6},{9,8},{10,9},{11,10},{13,12},{... | collective-permute-start | bytes 98312 | tf_op jit(solution)/shard_map/ppermute | solution.py:16
  138.3 12.8 %collective-permute-start.2 = (bf16[1,1,64,256]{3,2,1,0:T(8,128)(2,1)S(1)}, bf16[1,1,64,256]{3,2,1,0:T(8,128)(2,1)S(1)}, u32[]{:S(2)}, u32[]{:S(2)}) collective-permute-start(bf16[1,1,64,256]{3,2,1,0:T(8,128)(2,1)S(1)} %get-tuple-element.206), channel_id=1, source_target_pairs={{0,1},{1,2},{2,3},{4,5},{5,6},{6,7},{8,9},{9,10},{10,11},{12,13},{... | collective-permute-start | bytes 98312 | tf_op jit(solution)/shard_map/ppermute | solution.py:13
  153.1 1.1 copy-start.5
  153.4 1.3 copy-start.4
  161.0 0.9 copy-start.7
  161.0 1.2 copy-start.8
  161.2 1.2 copy-start.10
  294.3 2.5 copy-start.6
Sparse Core Ops, SparseCore 0:
  17.5 53.9 all-gather.3
  73.7 47.7 all-gather.5
  161.1 133.1 all-reduce.6
where the time goes:
time: 305 us; the launch traced here: 304 us
  waiting for transfers between devices  166 us (54%)
  blocking collectives  65.8 us (22%)
  starting transfers between devices  20.1 us (7%)
  other arithmetic  15.3 us (5%)
  between operations  14.4 us (5%)
  matrix products  13.9 us (5%)
  local copies, waits for them, and re-layouts  8.25 us (3%)
    psum x1, waiting for transfers between devices, on_device(): lax.psum((in_grad_terms, out_grad_terms, gain_terms), ('tm', 'rows'))  94 us
    all_gather x2, waiting for transfers between devices, entering(): lax.all_gather(a.astype(kind), axis)  71.4 us
    psum x1, blocking collectives, on_device(): lax.psum((in_grad_terms, out_grad_terms, gain_terms), ('tm', 'rows'))  37.1 us
    all_gather x1, blocking collectives, entering(): lax.all_gather(a.astype(kind), axis)  20.8 us
    ppermute x4, starting transfers between devices, padded_2(): lax.ppermute(lax.slice_in_dim(block, block.shape[dim] - width, None, axis...  14.8 us
    dot_general x36, matrix products, conv_taps(): jnp.dot(window, weights[row_tap, col_tap], preferred_element_type=jnp.flo...  9.44 us
    add x7, other arithmetic, combine(): later[0][None, None, :] * earlier[1] + later[1]  8.23 us
    psum x1, blocking collectives, on_device(): decay_grad = lax.psum(decay_terms, 'rows')  7.91 us
  transfers between devices with their start and end apart: 11, of which 5 were waited for; matrix products, arithmetic and copies ran while one was open for 3% of the time, Pallas kernels for 0%

commit v1 on v0

--- a/solution.py
+++ b/solution.py
@@ -146,7 +146,7 @@
         conv_taps(adjoint_pad, flipped(in_weight)) + skip_gain * cotangent.astype(jnp.float32)
     ).astype(jnp.bfloat16)
     in_weight_grad, out_weight_grad, gain_grad = lax.psum(
-        (in_grad_terms, out_grad_terms, gain_terms), ("tm", "rows")
+        lax.psum((in_grad_terms, out_grad_terms, gain_terms), "rows"), "tm"
     )
     decay_grad = lax.psum(decay_terms, "rows")
     return (output_frames, input_grad, in_weight_grad, out_weight_grad, gain_grad, decay_grad)

time: 305 us -> 331 us (1.085)
  waiting for transfers between devices: 166 us -> 207 us
  blocking collectives: 65.8 us -> 50.6 us
  local copies, waits for them, and re-layouts: 8.25 us -> 11.6 us
    psum x1 -> x2, waiting for transfers between devices: 94 us -> 141 us  [the longest x1 78.8 us: on_device(): lax.psum(lax.psum((in_grad_terms, out_grad_terms, gain_terms), 'rows'), '...]
    psum x2, blocking collectives: 45 us -> 29.8 us  [the longest x1 23.5 us: on_device(): lax.psum(lax.psum((in_grad_terms, out_grad_terms, gain_terms), 'rows'), '...]
    all_gather x2, waiting for transfers between devices: 71.4 us -> 61.6 us  [entering(): lax.all_gather(a.astype(kind), axis)]
    ppermute x4, waiting for transfers between devices: 0.01 us -> 4.56 us  [padded_2(): lax.ppermute(lax.slice_in_dim(block, 0, width, axis=dim), axis, backward)]
  transfers between devices with their start and end apart: 11 -> 12, of which waited for: 5 -> 6; matrix products, arithmetic and copies ran while one was open for 3% -> 7% of each run, Pallas kernels for 0% -> 0%
where the time goes in v1:
time: 331 us
  waiting for transfers between devices  207 us (63%)
  blocking collectives  50.6 us (15%)
  starting transfers between devices  18.2 us (5%)
  between operations  14.5 us (4%)
  other arithmetic  14.4 us (4%)
  matrix products  13.8 us (4%)
  local copies, waits for them, and re-layouts  11.6 us (4%)
    psum x1, waiting for transfers between devices, on_device(): lax.psum(lax.psum((in_grad_terms, out_grad_terms, gain_terms), 'rows'), '...  78.8 us
    psum x1, waiting for transfers between devices, on_device(): lax.psum((in_grad_terms, out_grad_terms, gain_terms), 'rows')  62.3 us
    all_gather x2, waiting for transfers between devices, entering(): lax.all_gather(a.astype(kind), axis)  61.6 us
    psum x1, blocking collectives, on_device(): lax.psum(lax.psum((in_grad_terms, out_grad_terms, gain_terms), 'rows'), '...  23.5 us
    all_gather x1, blocking collectives, entering(): lax.all_gather(a.astype(kind), axis)  20.8 us
    ppermute x4, starting transfers between devices, padded_2(): lax.ppermute(lax.slice_in_dim(block, block.shape[dim] - width, None, axis...  12.9 us
    dot_general x36, matrix products, conv_taps(): jnp.dot(window, weights[row_tap, col_tap], preferred_element_type=jnp.flo...  9.39 us
    add x7, other arithmetic, combine(): later[0][None, None, :] * earlier[1] + later[1]  8.23 us
  transfers between devices with their start and end apart: 12, of which 6 were waited for; matrix products, arithmetic and copies ran while one was open for 7% of the time, Pallas kernels for 0%

profile of v1, /device:TPU:0, one launch (start us, length us, event | category | flops | bytes accessed | tf_op | source)
XLA Modules:
  0.0 330.7 jit_solution(649604095282102272)
XLA Ops:
  8.0 2.3 collective-permute-start.4
  10.3 1.3 collective-permute-start.5
  12.8 2.8 collective-permute-done.5
  19.2 4.5 %collective-permute-start = (bf16[1,1,64,128]{3,2,1,0:T(8,128)(2,1)S(1)}, bf16[1,1,64,128]{3,2,1,0:T(8,128)(2,1)S(1)}, u32[]{:S(2)}, u32[]{:S(2)}) collective-permute-start(bf16[1,1,64,128]{3,2,1,0:T(8,128)(2,1)S(1)} %get-tuple-element.233), channel_id=1, source_target_pairs={{0,1},{1,2},{2,3},{4,5},{5,6},{6,7},{8,9},{9,10},{10,11},{12,13},{... | collective-permute-start | bytes 49160 | tf_op jit(solution)/shard_map/ppermute | solution.py:13
  23.7 1.3 collective-permute-start.1
  25.0 1.8 collective-permute-done.1
  29.8 20.8 %all-gather = bf16[8,1,256]{2,1,0:T(2,128)(2,1)S(1)} all-gather(bf16[1,1,256]{2,1,0:T(2,128)(2,1)S(1)} %convert_bitcast_fusion), channel_id=1, replica_groups=mesh['tm'=8,'rows'=4] {'tm'}, dimensions={0}, use_global_device_ids=true | all-gather | bytes 4608 | tf_op jit(solution)/shard_map/all_gather | solution.py:26
  51.5 19.6 %all-gather.6.cloned.1.call-done = bf16[8,8,64,256]{3,2,1,0:T(8,128)(2,1)} async-done(((bf16[1,8,64,256]{3,2,1,0:T(8,128)(2,1)}), bf16[8,8,64,256]{3,2,1,0:T(8,128)(2,1)}) %all-gather.6.cloned.1.call-update) | async-done | bytes 2097168 | tf_op jit(solution)/shard_map/all_gather | solution.py:26
  71.2 8.5 %while.17 = (s32[]{:T(128)}, f32[8,64,256]{2,1,0:T(8,128)S(1)}, s32[]{:T(128)}, bf16[8,256]{1,0:T(8,128)(2,1)S(1)}, bf16[8,8,64,256]{3,2,1,0:T(8,128)(2,1)}, /*index=5*/s32[]{:T(128)}, s32[]{:T(128)}, s32[]{:T(128)}, s32[]{:T(128)}) while((s32[]{:T(128)}, f32[8,64,256]{2,1,0:T(8,128)S(1)}, s32[]{:T(128)}, bf16[8,256]{1,0:T(8,128)(2,1)S(1)}, ...), condition=%wide.region_4.5_spmd, body=%wide.region_3.4_spmd.sunk | while | flops 393478 | bytes 1313427 | solution.py:41
  71.2 1.2 convert_add_fusion.5
  74.9 1.2 convert_add_fusion.5
  76.1 1.2 convert_add_fusion.5
  78.5 1.2 convert_add_fusion.5
  79.7 41.9 %all-gather.4.cloned.1.call-done = bf16[8,8,64,256]{3,2,1,0:T(8,128)(2,1)} async-done(((bf16[1,8,64,256]{3,2,1,0:T(8,128)(2,1)}), bf16[8,8,64,256]{3,2,1,0:T(8,128)(2,1)}) %all-gather.4.cloned.1.call-update) | async-done | bytes 2097168 | tf_op jit(solution)/shard_map/all_gather | solution.py:26
  124.3 1.3 collective-permute-start.2
  125.6 1.3 collective-permute-start.3
  126.9 4.7 %collective-permute-start.6 = (bf16[1,1,64,256]{3,2,1,0:T(8,128)(2,1)S(1)}, bf16[1,1,64,256]{3,2,1,0:T(8,128)(2,1)S(1)}, u32[]{:S(2)}, u32[]{:S(2)}) collective-permute-start(bf16[1,1,64,256]{3,2,1,0:T(8,128)(2,1)S(1)} %get-tuple-element.206), channel_id=1, source_target_pairs={{0,1},{1,2},{2,3},{4,5},{5,6},{6,7},{8,9},{9,10},{10,11},{12,13},{... | collective-permute-start | bytes 98312 | tf_op jit(solution)/shard_map/ppermute | solution.py:13
  131.7 1.3 collective-permute-start.7
  137.7 1.3 fusion.95
  145.4 62.3 %all-reduce.12.cloned.1.call-done = (f32[3,3,128,256]{3,2,1,0:T(8,128)}, f32[3,3,256,128]{3,2,1,0:T(8,128)}) async-done(((f32[3,3,128,256]{3,2,1,0:T(8,128)}, f32[3,3,256,128]{3,2,1,0:T(8,128)}), (f32[3,3,128,256]{3,2,1,0:T(8,128)}, f32[3,3,256,128]{3,2,1,0:T(8,128)})) %all-reduce.12.cloned.1.call-update) | async-done | bytes 2359312 | tf_op jit(solution)/shard_map/psum | solution.py:149
  212.1 6.3 %all-reduce.5 = (f32[128]{0:T(128)S(1)}, f32[1,256]{1,0:T(1,128)}) all-reduce(f32[128]{0:T(128)S(1)} %broadcast_multiply_fusion.2, f32[1,256]{1,0:T(1,128)S(1)} %bitcast.421), channel_id=1, replica_groups=mesh['tm'=8,'rows'=4] {'rows'}, use_global_device_ids=true, to_apply=%region_10.11 | all-reduce | flops 384 | bytes 3072 | tf_op jit(solution)/shard_map/psum | solution.py:149
  218.4 23.5 %psum.54 = f32[128]{0:T(128)} all-reduce(f32[128]{0:T(128)S(1)} %get-tuple-element.185), channel_id=1, replica_groups=mesh['tm'=8,'rows'=4] {'tm'}, use_global_device_ids=true, to_apply=%region_11.12 | all-reduce | flops 128 | bytes 1024 | tf_op jit(solution)/shard_map/psum | solution.py:148
  241.9 78.8 %all-reduce.10.cloned.1.call-done = (f32[3,3,128,256]{3,2,1,0:T(8,128)}, f32[3,3,256,128]{3,2,1,0:T(8,128)}) async-done(((f32[3,3,128,256]{3,2,1,0:T(8,128)}, f32[3,3,256,128]{3,2,1,0:T(8,128)}), (f32[3,3,128,256]{3,2,1,0:T(8,128)}, f32[3,3,256,128]{3,2,1,0:T(8,128)})) %all-reduce.10.cloned.1.call-update) | async-done | bytes 2359312 | tf_op jit(solution)/shard_map/psum | solution.py:148
  320.7 2.5 copy.36
  (153 shorter events, 31.6 us)
Async XLA Ops:
  7.2 8.4 %copy-start = (bf16[1,8,64,128]{3,2,1,0:T(8,128)(2,1)S(1)}, bf16[1,8,64,128]{3,2,1,0:T(8,128)(2,1)}, u32[]{:S(2)}) copy-start(bf16[1,8,64,128]{3,2,1,0:T(8,128)(2,1)} %param.15) | copy-start | bytes 393220
  7.2 64.0 %all-gather.6.cloned.1.call-start = ((), (), s32[]{:S(2)}) async-start(), calls=%async_computation.1 | async-start | bytes 2359296 | tf_op jit(solution)/shard_map/all_gather | solution.py:26
  8.0 4.8 %collective-permute-start.4 = (bf16[1,1,64,128]{3,2,1,0:T(8,128)(2,1)S(1)}, bf16[1,1,64,128]{3,2,1,0:T(8,128)(2,1)S(1)}, u32[]{:S(2)}, u32[]{:S(2)}) collective-permute-start(bf16[1,1,64,128]{3,2,1,0:T(8,128)(2,1)S(1)} %get-tuple-element.229), channel_id=1, source_target_pairs={{0,1},{1,2},{2,3},{4,5},{5,6},{6,7},{8,9},{9,10},{10,11},{12,13},{... | collective-permute-start | bytes 49160 | tf_op jit(solution)/shard_map/ppermute | solution.py:13
  10.3 5.2 %collective-permute-start.5 = (bf16[1,1,64,128]{3,2,1,0:T(8,128)(2,1)S(1)}, bf16[1,1,64,128]{3,2,1,0:T(8,128)(2,1)S(1)}, u32[]{:S(2)}, u32[]{:S(2)}) collective-permute-start(bf16[1,1,64,128]{3,2,1,0:T(8,128)(2,1)S(1)} %get-tuple-element.230), channel_id=1, source_target_pairs={{1,0},{2,1},{3,2},{5,4},{6,5},{7,6},{9,8},{10,9},{11,10},{13,12},{... | collective-permute-start | bytes 49160 | tf_op jit(solution)/shard_map/ppermute | solution.py:16
  17.7 1.5 copy-start.1
  19.1 102.5 %all-gather.4.cloned.1.call-start = ((), (), s32[]{:S(2)}) async-start(), calls=%async_computation | async-start | bytes 2359296 | tf_op jit(solution)/shard_map/all_gather | solution.py:26
  19.2 7.8 %copy-start.2 = (bf16[3,3,128,256]{3,2,1,0:T(8,128)(2,1)S(1)}, bf16[3,3,128,256]{3,2,1,0:T(8,128)(2,1)}, u32[]{:S(2)}) copy-start(bf16[3,3,128,256]{3,2,1,0:T(8,128)(2,1)} %param.12) | copy-start | bytes 1769476
  19.2 5.8 %collective-permute-start = (bf16[1,1,64,128]{3,2,1,0:T(8,128)(2,1)S(1)}, bf16[1,1,64,128]{3,2,1,0:T(8,128)(2,1)S(1)}, u32[]{:S(2)}, u32[]{:S(2)}) collective-permute-start(bf16[1,1,64,128]{3,2,1,0:T(8,128)(2,1)S(1)} %get-tuple-element.233), channel_id=1, source_target_pairs={{0,1},{1,2},{2,3},{4,5},{5,6},{6,7},{8,9},{9,10},{10,11},{12,13},{... | collective-permute-start | bytes 49160 | tf_op jit(solution)/shard_map/ppermute | solution.py:13
  23.7 3.1 collective-permute-start.1
  29.8 177.9 %all-reduce.12.cloned.1.call-start = ((), (), s32[]{:S(2)}) async-start(), calls=%async_computation.3 | async-start | bytes 4718592 | tf_op jit(solution)/shard_map/psum | solution.py:149
  124.3 9.9 %collective-permute-start.2 = (bf16[1,1,64,256]{3,2,1,0:T(8,128)(2,1)S(1)}, bf16[1,1,64,256]{3,2,1,0:T(8,128)(2,1)S(1)}, u32[]{:S(2)}, u32[]{:S(2)}) collective-permute-start(bf16[1,1,64,256]{3,2,1,0:T(8,128)(2,1)S(1)} %get-tuple-element.210), channel_id=1, source_target_pairs={{0,1},{1,2},{2,3},{4,5},{5,6},{6,7},{8,9},{9,10},{10,11},{12,13},{... | collective-permute-start | bytes 98312 | tf_op jit(solution)/shard_map/ppermute | solution.py:13
  125.6 8.6 %collective-permute-start.3 = (bf16[1,1,64,256]{3,2,1,0:T(8,128)(2,1)S(1)}, bf16[1,1,64,256]{3,2,1,0:T(8,128)(2,1)S(1)}, u32[]{:S(2)}, u32[]{:S(2)}) collective-permute-start(bf16[1,1,64,256]{3,2,1,0:T(8,128)(2,1)S(1)} %get-tuple-element.211), channel_id=1, source_target_pairs={{1,0},{2,1},{3,2},{5,4},{6,5},{7,6},{9,8},{10,9},{11,10},{13,12},{... | collective-permute-start | bytes 98312 | tf_op jit(solution)/shard_map/ppermute | solution.py:16
  126.9 10.7 %collective-permute-start.6 = (bf16[1,1,64,256]{3,2,1,0:T(8,128)(2,1)S(1)}, bf16[1,1,64,256]{3,2,1,0:T(8,128)(2,1)S(1)}, u32[]{:S(2)}, u32[]{:S(2)}) collective-permute-start(bf16[1,1,64,256]{3,2,1,0:T(8,128)(2,1)S(1)} %get-tuple-element.206), channel_id=1, source_target_pairs={{0,1},{1,2},{2,3},{4,5},{5,6},{6,7},{8,9},{9,10},{10,11},{12,13},{... | collective-permute-start | bytes 98312 | tf_op jit(solution)/shard_map/ppermute | solution.py:13
  131.7 5.9 %collective-permute-start.7 = (bf16[1,1,64,256]{3,2,1,0:T(8,128)(2,1)S(1)}, bf16[1,1,64,256]{3,2,1,0:T(8,128)(2,1)S(1)}, u32[]{:S(2)}, u32[]{:S(2)}) collective-permute-start(bf16[1,1,64,256]{3,2,1,0:T(8,128)(2,1)S(1)} %get-tuple-element.207), channel_id=1, source_target_pairs={{1,0},{2,1},{3,2},{5,4},{6,5},{7,6},{9,8},{10,9},{11,10},{13,12},{... | collective-permute-start | bytes 98312 | tf_op jit(solution)/shard_map/ppermute | solution.py:16
  135.8 1.1 copy-start.3
  142.2 1.2 copy-start.4
  142.2 1.3 copy-start.14
  142.2 1.7 copy-start.12
  142.2 178.5 %all-reduce.10.cloned.1.call-start = ((), (), s32[]{:S(2)}) async-start(), calls=%async_computation.2 | async-start | bytes 4718592 | tf_op jit(solution)/shard_map/psum | solution.py:148
  142.3 1.4 copy-start.16
  143.0 1.2 copy-start.11
  207.7 1.2 copy-start.9
  207.7 1.4 copy-start.8
  320.7 2.5 copy-start.5
  (7 other events, 6.5 us)
Sparse Core Ops, SparseCore 0:
  19.2 51.8 all-gather.5
  73.8 47.7 all-gather.3
  142.3 65.3 all-reduce.11
  211.2 109.4 all-reduce.9
